TPU v7x, 32 devices: a whole 2x2x4 slice. The times are simulated.
32 devices in a mesh: sim: 2 (over y), grp: 4 (over z), gz: 4 (over x, core).
Axes of the slice: x: 2, y: 2, z: 4, core: 2. Of those that a mesh axis runs over, the one named last changes fastest.
Arguments:
- fields: float32 [8, 2, 1024, 1024], P(None, None, 'sim', ('grp', 'gz')), may hold values from -6 to 6
- diffusivity: float32 [8], replicated, may hold values from 0.03 to 0.12
- velocity: float32 [2, 8], replicated, may hold values from -0.4 to 0.4
- coupling: float32 [8, 8], replicated, may hold values from -0.6 to 0.6
- basis_x: bfloat16 [1024, 128], replicated, may hold values from -0.1875 to 0.1875
- basis_y: bfloat16 [1024, 128], replicated, may hold values from -0.1875 to 0.1875
Outputs:
- fields_out: float32 [8, 2, 1024, 1024], P(None, None, 'sim', ('grp', 'gz'))
- gram_x: float32 [1024, 1024], P('sim', ('grp', 'gz'))
- gram_y: float32 [1024, 1024], P(('grp', 'gz'), 'sim')
- core: float32 [8, 2, 128, 128], P(None, None, 'sim', ('grp', 'gz'))
All inputs are finite; a program needn't handle non-finite values.
Results may differ from a plain program's by a relative error of at most 0.0003.
Values sent between devices are 32-bit elements; how exact they have to be, the bound alone decides.
No kernel may reach another device: no remote copies, remote signals or barrier semaphores. Data moves between devices by JAX's collectives and lax.ppermute only.
A program may use at most 64 MiB of HBM per device.

v0:
```python
import jax
import jax.numpy as jnp
from jax import lax
from jax.sharding import PartitionSpec as P

NY = 1024
RANK = 128
STEPS = 2
time_step = 1.0
highest = lax.Precision.HIGHEST


def with_halo(cells, sides, width):
    for axis, dim in sides:
        count = lax.axis_size(axis)
        head = lax.slice_in_dim(cells, 0, width, axis=dim)
        tail = lax.slice_in_dim(cells, cells.shape[dim] - width, cells.shape[dim], axis=dim)
        cells = jnp.concatenate(
            [
                lax.ppermute(tail, axis, [(i, (i + 1) % count) for i in range(count)]),
                cells,
                lax.ppermute(head, axis, [((i + 1) % count, i) for i in range(count)]),
            ],
            axis=dim,
        )
    return cells


def rates(state, diffusivity, velocity, coupling):
    padded = with_halo(state, (("sim", 2), (("grp", "gz"), 3)), 1)
    center = padded[:, :, 1:-1, 1:-1]
    x_plus = padded[:, :, 2:, 1:-1]
    x_minus = padded[:, :, :-2, 1:-1]
    y_plus = padded[:, :, 1:-1, 2:]
    y_minus = padded[:, :, 1:-1, :-2]
    z_plus = jnp.roll(center, -1, 1)
    z_minus = jnp.roll(center, 1, 1)
    lapl = -6.0 * center + z_plus + z_minus + x_plus + x_minus + y_plus + y_minus
    grad_x = (x_plus - x_minus) * 0.5
    grad_y = (y_plus - y_minus) * 0.5
    react = jnp.einsum("fg,gzxy->fzxy", coupling, jnp.tanh(center), precision=highest)
    return (
        diffusivity[:, None, None, None] * lapl
        - velocity[0][:, None, None, None] * grad_x
        - velocity[1][:, None, None, None] * grad_y
        + react
    )


def shards(fields, diffusivity, velocity, coupling, basis_x, basis_y):
    state = fields
    for repeat in range(STEPS):
        first = rates(state, diffusivity, velocity, coupling)
        second = rates(state + 0.5 * time_step * first, diffusivity, velocity, coupling)
        third = rates(state + 0.5 * time_step * second, diffusivity, velocity, coupling)
        fourth = rates(state + time_step * third, diffusivity, velocity, coupling)
        state = state + time_step / 6.0 * (first + 2.0 * second + 2.0 * third + fourth)
    nfield = state.shape[0]
    depth = state.shape[1]
    x_rows = state.shape[2]
    basis_xf = basis_x.astype(jnp.float32)
    basis_yf = basis_y.astype(jnp.float32)
    block = jnp.einsum(
        "fzxy,fzwy->xw", state, lax.all_gather(state, "sim", axis=2, tiled=True), precision=highest
    )
    gram_rows = block
    own_basis = lax.dynamic_slice_in_dim(basis_xf, lax.axis_index("sim") * x_rows, x_rows, 0)
    partial_proj = jnp.einsum("xr,fzxy->fzry", own_basis, state, precision=highest)
    projected = lax.psum_scatter(partial_proj, "sim", scatter_dimension=2, tiled=True)
    gram_x = lax.psum_scatter(gram_rows, ("grp", "gz"), scatter_dimension=1, tiled=True) / (
        nfield * depth * NY
    )
    rank_grp = RANK // lax.axis_size(("grp", "gz"))
    rank_cols_y = lax.dynamic_slice_in_dim(
        basis_yf, lax.axis_index(("grp", "gz")) * rank_grp, rank_grp, 1
    )
    incoming = lax.all_gather(projected, ("grp", "gz"), axis=3, tiled=True)
    block = jnp.einsum("fzry,fzrv->yv", projected, incoming, precision=highest)
    core_part = jnp.einsum("vs,fzrv->fzrs", rank_cols_y, incoming, precision=highest)
    gram_y = lax.psum_scatter(block, "sim", scatter_dimension=1, tiled=True) / (
        nfield * depth * RANK
    )
    return (state, gram_x, gram_y, core_part)


def solution(mesh):
    in_specs = (P(None, None, "sim", ("grp", "gz")), P(), P(), P(), P(), P())
    out_specs = (
        P(None, None, "sim", ("grp", "gz")),
        P("sim", ("grp", "gz")),
        P(("grp", "gz"), "sim"),
        P(None, None, "sim", ("grp", "gz")),
    )
    return jax.shard_map(shards, mesh=mesh, in_specs=in_specs, out_specs=out_specs, check_vma=False)
```

profile of v0, /device:TPU:0, one launch (start us, length us, event | category | flops | bytes accessed | tf_op | source)
XLA Modules:
  0.0 532.1 jit_solution(15932883289345783442)
XLA Ops:
  7.2 2.8 copy.61
  10.3 3.1 collective-permute-start
  13.6 12.5 %collective-permute-done = f32[8,2,1,64]{2,0,3,1:T(8,128)S(1)} collective-permute-done((f32[8,2,1,64]{2,0,3,1:T(8,128)S(1)}, f32[8,2,1,64]{2,0,3,1:T(8,128)S(1)}, u32[]{:S(2)}, u32[]{:S(2)}) %collective-permute-start) | collective-permute-done | bytes 4128 | tf_op jit(solution)/shard_map/ppermute | solution.py:22
  26.1 10.4 %collective-permute-done.1 = f32[8,2,1,64]{2,0,3,1:T(8,128)S(1)} collective-permute-done((f32[8,2,1,64]{2,0,3,1:T(8,128)S(1)}, f32[8,2,1,64]{2,0,3,1:T(8,128)S(1)}, u32[]{:S(2)}, u32[]{:S(2)}) %collective-permute-start.1) | collective-permute-done | bytes 4128 | tf_op jit(solution)/shard_map/ppermute | solution.py:20
  36.6 3.4 collective-permute-start.2
  41.6 4.4 collective-permute-done.3
  46.1 5.2 multiply_add_fusion.3
  51.5 1.6 collective-permute-start.4
  53.6 12.5 %collective-permute-done.4 = f32[8,2,1,64]{2,0,3,1:T(8,128)S(1)} collective-permute-done((f32[8,2,1,64]{2,0,3,1:T(8,128)S(1)}, f32[8,2,1,64]{2,0,3,1:T(8,128)S(1)}, u32[]{:S(2)}, u32[]{:S(2)}) %collective-permute-start.4) | collective-permute-done | bytes 4128 | tf_op jit(solution)/shard_map/ppermute | solution.py:22
  66.1 5.6 %collective-permute-done.5 = f32[8,2,1,64]{2,0,3,1:T(8,128)S(1)} collective-permute-done((f32[8,2,1,64]{2,0,3,1:T(8,128)S(1)}, f32[8,2,1,64]{2,0,3,1:T(8,128)S(1)}, u32[]{:S(2)}, u32[]{:S(2)}) %collective-permute-start.5) | collective-permute-done | bytes 4128 | tf_op jit(solution)/shard_map/ppermute | solution.py:20
  71.9 4.1 collective-permute-start.6
  77.7 4.6 collective-permute-done.7
  82.3 4.5 multiply_add_fusion.2
  87.0 1.6 collective-permute-start.8
  89.1 12.5 %collective-permute-done.8 = f32[8,2,1,64]{2,0,3,1:T(8,128)S(1)} collective-permute-done((f32[8,2,1,64]{2,0,3,1:T(8,128)S(1)}, f32[8,2,1,64]{2,0,3,1:T(8,128)S(1)}, u32[]{:S(2)}, u32[]{:S(2)}) %collective-permute-start.8) | collective-permute-done | bytes 4128 | tf_op jit(solution)/shard_map/ppermute | solution.py:22
  101.6 5.6 %collective-permute-done.9 = f32[8,2,1,64]{2,0,3,1:T(8,128)S(1)} collective-permute-done((f32[8,2,1,64]{2,0,3,1:T(8,128)S(1)}, f32[8,2,1,64]{2,0,3,1:T(8,128)S(1)}, u32[]{:S(2)}, u32[]{:S(2)}) %collective-permute-start.9) | collective-permute-done | bytes 4128 | tf_op jit(solution)/shard_map/ppermute | solution.py:20
  107.3 2.7 collective-permute-start.10
  110.2 1.5 collective-permute-done.10
  111.7 4.4 collective-permute-done.11
  116.1 4.9 copy_add_fusion
  121.2 1.6 collective-permute-start.12
  123.3 12.5 %collective-permute-done.12 = f32[8,2,1,64]{2,0,3,1:T(8,128)S(1)} collective-permute-done((f32[8,2,1,64]{2,0,3,1:T(8,128)S(1)}, f32[8,2,1,64]{2,0,3,1:T(8,128)S(1)}, u32[]{:S(2)}, u32[]{:S(2)}) %collective-permute-start.12) | collective-permute-done | bytes 4128 | tf_op jit(solution)/shard_map/ppermute | solution.py:22
  135.8 5.6 %collective-permute-done.13 = f32[8,2,1,64]{2,0,3,1:T(8,128)S(1)} collective-permute-done((f32[8,2,1,64]{2,0,3,1:T(8,128)S(1)}, f32[8,2,1,64]{2,0,3,1:T(8,128)S(1)}, u32[]{:S(2)}, u32[]{:S(2)}) %collective-permute-start.13) | collective-permute-done | bytes 4128 | tf_op jit(solution)/shard_map/ppermute | solution.py:20
  144.5 4.6 collective-permute-done.15
  149.2 5.1 fusion.36
  154.5 1.6 collective-permute-start.16
  156.6 12.5 %collective-permute-done.16 = f32[8,2,1,64]{2,0,3,1:T(8,128)S(1)} collective-permute-done((f32[8,2,1,64]{2,0,3,1:T(8,128)S(1)}, f32[8,2,1,64]{2,0,3,1:T(8,128)S(1)}, u32[]{:S(2)}, u32[]{:S(2)}) %collective-permute-start.16) | collective-permute-done | bytes 4128 | tf_op jit(solution)/shard_map/ppermute | solution.py:22
  169.1 5.6 %collective-permute-done.17 = f32[8,2,1,64]{2,0,3,1:T(8,128)S(1)} collective-permute-done((f32[8,2,1,64]{2,0,3,1:T(8,128)S(1)}, f32[8,2,1,64]{2,0,3,1:T(8,128)S(1)}, u32[]{:S(2)}, u32[]{:S(2)}) %collective-permute-start.17) | collective-permute-done | bytes 4128 | tf_op jit(solution)/shard_map/ppermute | solution.py:20
  176.0 1.5 collective-permute-done.18
  177.5 4.4 collective-permute-done.19
  181.9 5.4 %multiply_add_fusion.1 = (f32[8,2,512,64]{2,0,3,1:T(8,128)S(1)}, f32[8,2,512,64]{2,0,3,1:T(8,128)}) fusion(f32[8,2,512,64]{2,0,3,1:T(8,128)S(1)} %fusion.36, f32[8,8]{1,0:T(8,128)S(1)} %copy-done.9, f32[8]{0:T(128)S(1)} %get-tuple-element.65, f32[8]{0:T(128)S(1)} %get-tuple-element.64, f32[8,2,1,64]{2,0,3,1:T(8,128)S(1)} %collective-permute-done.16, ...), kind=kOutput, calls=%fused_computation.154 | convolution fusion | flops 63963136 | bytes 8462944 | tf_op jit(solution)/shard_map/fg,gzxy->fzxy/dot_general | solution.py:41
  187.5 1.6 collective-permute-start.20
  189.6 12.5 %collective-permute-done.20 = f32[8,2,1,64]{2,0,3,1:T(8,128)S(1)} collective-permute-done((f32[8,2,1,64]{2,0,3,1:T(8,128)S(1)}, f32[8,2,1,64]{2,0,3,1:T(8,128)S(1)}, u32[]{:S(2)}, u32[]{:S(2)}) %collective-permute-start.20) | collective-permute-done | bytes 4128 | tf_op jit(solution)/shard_map/ppermute | solution.py:22
  202.1 5.6 %collective-permute-done.21 = f32[8,2,1,64]{2,0,3,1:T(8,128)S(1)} collective-permute-done((f32[8,2,1,64]{2,0,3,1:T(8,128)S(1)}, f32[8,2,1,64]{2,0,3,1:T(8,128)S(1)}, u32[]{:S(2)}, u32[]{:S(2)}) %collective-permute-start.21) | collective-permute-done | bytes 4128 | tf_op jit(solution)/shard_map/ppermute | solution.py:20
  209.2 1.5 collective-permute-done.22
  210.7 4.4 collective-permute-done.23
  215.1 5.5 %multiply_add_fusion = (f32[8,2,512,64]{2,0,3,1:T(8,128)S(1)}, f32[8,2,512,64]{2,0,3,1:T(8,128)}) fusion(f32[8,2,512,64]{2,0,3,1:T(8,128)S(1)} %fusion.36, f32[8,8]{1,0:T(8,128)S(1)} %copy-done.9, f32[8,2,512,64]{2,0,3,1:T(8,128)S(1)} %get-tuple-element.72, f32[8]{0:T(128)S(1)} %get-tuple-element.65, f32[8]{0:T(128)S(1)} %get-tuple-element.64, ...), kind=kOutput, calls=%fused_computation.151 | convolution fusion | flops 63963136 | bytes 10560096 | tf_op jit(solution)/shard_map/fg,gzxy->fzxy/dot_general | solution.py:41
  220.9 1.6 collective-permute-start.24
  223.0 12.5 %collective-permute-done.24 = f32[8,2,1,64]{2,0,3,1:T(8,128)S(1)} collective-permute-done((f32[8,2,1,64]{2,0,3,1:T(8,128)S(1)}, f32[8,2,1,64]{2,0,3,1:T(8,128)S(1)}, u32[]{:S(2)}, u32[]{:S(2)}) %collective-permute-start.24) | collective-permute-done | bytes 4128 | tf_op jit(solution)/shard_map/ppermute | solution.py:22
  235.5 5.6 %collective-permute-done.25 = f32[8,2,1,64]{2,0,3,1:T(8,128)S(1)} collective-permute-done((f32[8,2,1,64]{2,0,3,1:T(8,128)S(1)}, f32[8,2,1,64]{2,0,3,1:T(8,128)S(1)}, u32[]{:S(2)}, u32[]{:S(2)}) %collective-permute-start.25) | collective-permute-done | bytes 4128 | tf_op jit(solution)/shard_map/ppermute | solution.py:20
  241.2 1.9 collective-permute-start.26
  244.8 4.8 collective-permute-done.27
  249.7 5.6 %fusion.158 = (f32[8,2,512,64]{2,0,3,1:T(8,128)S(1)}, f32[8,2,512,64]{2,0,3,1:T(8,128)}) fusion(f32[8,2,512,64]{2,0,3,1:T(8,128)S(1)} %fusion.36, f32[8,8]{1,0:T(8,128)S(1)} %copy-done.9, f32[8,2,512,64]{2,0,3,1:T(8,128)S(1)} %get-tuple-element.74, f32[8]{0:T(128)S(1)} %get-tuple-element.65, f32[8]{0:T(128)S(1)} %get-tuple-element.64, ...), kind=kOutput, calls=%fused_computation.229 | convolution fusion | flops 63438848 | bytes 10560096 | tf_op jit(solution)/shard_map/fg,gzxy->fzxy/dot_general | solution.py:41
  256.6 1.5 collective-permute-start.28
  258.7 12.7 %collective-permute-done.28 = f32[8,2,1,64]{2,0,3,1:T(8,128)S(1)} collective-permute-done((f32[8,2,1,64]{2,0,3,1:T(8,128)}, f32[8,2,1,64]{2,0,3,1:T(8,128)S(1)}, u32[]{:S(2)}, u32[]{:S(2)}) %collective-permute-start.28) | collective-permute-done | bytes 4128 | tf_op jit(solution)/shard_map/ppermute | solution.py:22
  271.4 5.6 %collective-permute-done.29 = f32[8,2,1,64]{2,0,3,1:T(8,128)S(1)} collective-permute-done((f32[8,2,1,64]{2,0,3,1:T(8,128)}, f32[8,2,1,64]{2,0,3,1:T(8,128)S(1)}, u32[]{:S(2)}, u32[]{:S(2)}) %collective-permute-start.29) | collective-permute-done | bytes 4128 | tf_op jit(solution)/shard_map/ppermute | solution.py:20
  277.1 1.8 collective-permute-start.30
  280.5 4.5 collective-permute-done.31
  285.0 8.8 %fusion.71 = f32[8,2,512,64]{2,0,3,1:T(8,128)S(1)} fusion(f32[8,2,512,64]{2,0,3,1:T(8,128)S(1)} %copy-done.4, f32[8,1,512,64]{2,0,3,1:T(8,128)S(1)} %get-tuple-element.35, f32[8,1,512,64]{2,0,3,1:T(8,128)S(1)} %get-tuple-element.34, f32[8,2,514,1]{2,0,3,1:T(8,128)S(1)} %collective-permute-done.30, f32[8,2,1,64]{2,0,3,1:T(8,128)S(1)} %collective-permute-done.28, ...), kind=kOutput, calls=%fused_computation.79 | convolution fusion | flops 66584576 | bytes 14754400 | tf_op jit(solution)/shard_map/fg,gzxy->fzxy/dot_general | solution.py:41
  293.9 1.9 convolution_bitcast_fusion
  295.8 1.9 copy.75
  297.7 1.8 reshape.20
  300.3 11.4 %reduce-scatter.10.cloned.1.call-done = f32[64,1024]{1,0:T(8,128)} async-done(((f32[128,1024]{1,0:T(8,128)}), f32[64,1024]{1,0:T(8,128)}) %reduce-scatter.10.cloned.1.call-update) | async-done | bytes 262160
  314.5 56.1 %all-gather.3.cloned.1.call-done = f32[8,2,1024,64]{2,0,3,1:T(8,128)} async-done(((f32[8,2,512,64]{2,0,3,1:T(8,128)}), f32[8,2,1024,64]{2,0,3,1:T(8,128)}) %all-gather.3.cloned.1.call-update) | async-done | bytes 4194320 | tf_op jit(solution)/shard_map/all_gather | solution.py:64
  370.5 9.7 %fusion.89 = f32[512,1024]{0,1:T(8,128)} fusion(f32[8,2,1024,64]{2,0,3,1:T(8,128)} %all-gather.3.cloned.1.call-done, f32[8,2,512,64]{2,0,3,1:T(8,128)S(1)} %copy-done.2), kind=kOutput, calls=%fused_computation.165 | convolution fusion | flops 6442450944 | bytes 8388608 | tf_op jit(solution)/shard_map/fzxy,fzwy->xw/dot_general | solution.py:63
  380.3 2.5 copy.69
  382.8 64.2 %all-gather.5.cloned.1.call-done = f32[8,2,64,1024]{2,0,1,3:T(8,128)} async-done(((f32[8,2,64,64]{2,0,1,3:T(8,128)}), f32[8,2,64,1024]{2,0,1,3:T(8,128)}) %all-gather.5.cloned.1.call-update) | async-done | bytes 4194320 | tf_op jit(solution)/shard_map/all_gather | solution.py:77
  447.0 6.9 %copy.66 = f32[8,2,64,1024]{3,2,1,0:T(8,128)} copy(f32[8,2,64,1024]{2,0,1,3:T(8,128)} %all-gather.5.cloned.1.call-done) | data formatting | bytes 8388608 | tf_op jit(solution)/shard_map/all_gather | solution.py:77
  453.9 5.8 %convolution_bitcast_fusion.1 = f32[64,1024]{1,0:T(8,128)} fusion(f32[8,2,64,1024]{3,2,1,0:T(8,128)} %copy.66, f32[8,2,64,64]{3,1,0,2:T(2,128)S(1)} %bitcast.93), kind=kOutput, calls=%fused_computation.167 | convolution fusion | flops 805306368 | bytes 4718592 | tf_op jit(solution)/shard_map/fzry,fzrv->yv/dot_general | solution.py:78
  459.7 51.4 %reduce-scatter.6.cloned.1.call-done = f32[512,64]{0,1:T(8,128)} async-done(((f32[512,1024]{0,1:T(8,128)}), f32[512,64]{0,1:T(8,128)}) %reduce-scatter.6.cloned.1.call-update) | async-done | bytes 131088 | tf_op jit(solution)/shard_map/reduce_scatter | solution.py:70
  511.0 1.6 broadcast_multiply_fusion.1
  512.6 5.5 %fusion.95 = f32[8,2,64,8]{2,3,1,0:T(8,128)} fusion(f32[8,2,64,1024]{3,2,1,0:T(8,128)} %copy.66, bf16[1024,128]{1,0:T(8,128)(2,1)S(1)} %copy-done.7, s32[]{:T(128)S(6)} %select_n.7), kind=kOutput, calls=%fused_computation.169 | convolution fusion | flops 100663296 | bytes 4489220 | tf_op jit(solution)/shard_map/vs,fzrv->fzrs/dot_general | solution.py:79
  518.0 5.8 %reduce-scatter.8.cloned.1.call-done = f32[64,512]{1,0:T(8,128)} async-done(((f32[64,1024]{1,0:T(8,128)}), f32[64,512]{1,0:T(8,128)}) %reduce-scatter.8.cloned.1.call-update) | async-done | bytes 131088 | tf_op jit(solution)/shard_map/reduce_scatter | solution.py:80
  523.8 1.6 broadcast_multiply_fusion
  (88 shorter events, 23.2 us)
Async XLA Ops:
  7.2 286.7 %copy-start = (bf16[1024,128]{1,0:T(8,128)(2,1)S(1)}, bf16[1024,128]{1,0:T(8,128)(2,1)}, u32[]{:S(2)}) copy-start(bf16[1024,128]{1,0:T(8,128)(2,1)} %param.10) | copy-start | bytes 786436
  7.2 304.5 %reduce-scatter.10.cloned.1.call-start = ((), (), s32[]{:S(2)}) async-start(), calls=%async_computation.7 | async-start | bytes 786432
  10.3 15.8 %collective-permute-start = (f32[8,2,1,64]{2,0,3,1:T(8,128)S(1)}, f32[8,2,1,64]{2,0,3,1:T(8,128)S(1)}, u32[]{:S(2)}, u32[]{:S(2)}) collective-permute-start(f32[8,2,1,64]{2,0,3,1:T(8,128)S(1)} %get-tuple-element.61), channel_id=1, source_target_pairs={{16,0},{0,16},{17,1},{1,17},{18,2},{2,18},{19,3},{3,19},{20,4},{4,... | collective-permute-start | bytes 12296 | tf_op jit(solution)/shard_map/ppermute | solution.py:22
  13.3 23.2 %collective-permute-start.1 = (f32[8,2,1,64]{2,0,3,1:T(8,128)S(1)}, f32[8,2,1,64]{2,0,3,1:T(8,128)S(1)}, u32[]{:S(2)}, u32[]{:S(2)}) collective-permute-start(f32[8,2,1,64]{2,0,3,1:T(8,128)S(1)} %get-tuple-element.60), channel_id=1, source_target_pairs={{0,16},{16,0},{1,17},{17,1},{2,18},{18,2},{3,19},{19,3},{4,20},{20... | collective-permute-start | bytes 12296 | tf_op jit(solution)/shard_map/ppermute | solution.py:20
  13.6 26.4 %copy-start.8 = (f32[2,8]{1,0:T(2,128)S(1)}, f32[2,8]{1,0:T(2,128)}, u32[]{:S(2)}) copy-start(f32[2,8]{1,0:T(2,128)} %param.8) | copy-start | bytes 196
  13.6 26.4 %copy-start.6 = (f32[8,2,512,64]{2,3,1,0:T(8,128)S(1)}, f32[8,2,512,64]{2,3,1,0:T(8,128)}, u32[]{:S(2)}) copy-start(f32[8,2,512,64]{2,3,1,0:T(8,128)} %param.6) | copy-start | bytes 6291460
  36.6 5.1 collective-permute-start.2
  40.0 6.1 %collective-permute-start.3 = (f32[8,2,514,1]{2,0,3,1:T(8,128)S(1)}, f32[8,2,514,1]{2,0,3,1:T(8,128)S(1)}, u32[]{:S(2)}, u32[]{:S(2)}) collective-permute-start(f32[8,2,514,1]{2,0,3,1:T(8,128)S(1)} %get-tuple-element.30), channel_id=1, source_target_pairs={{0,1},{1,2},{2,3},{3,4},{4,5},{5,6},{6,7},{7,8},{8,9},{9,10},{10,1... | collective-permute-start | bytes 98696 | tf_op jit(solution)/shard_map/ppermute | solution.py:20
  40.0 6.1 %copy-start.9 = (f32[8,8]{1,0:T(8,128)S(1)}, f32[8,8]{1,0:T(8,128)}, u32[]{:S(2)}) copy-start(f32[8,8]{1,0:T(8,128)} %param.9) | copy-start | bytes 772
  40.0 6.1 %copy-start.10 = (f32[8]{0:T(128)S(1)}, f32[8]{0:T(128)}, u32[]{:S(2)}) copy-start(f32[8]{0:T(128)} %param.7) | copy-start | bytes 100
  51.5 14.6 %collective-permute-start.4 = (f32[8,2,1,64]{2,0,3,1:T(8,128)S(1)}, f32[8,2,1,64]{2,0,3,1:T(8,128)S(1)}, u32[]{:S(2)}, u32[]{:S(2)}) collective-permute-start(f32[8,2,1,64]{2,0,3,1:T(8,128)S(1)} %get-tuple-element.57), channel_id=1, source_target_pairs={{16,0},{0,16},{17,1},{1,17},{18,2},{2,18},{19,3},{3,19},{20,4},{4,... | collective-permute-start | bytes 12296 | tf_op jit(solution)/shard_map/ppermute | solution.py:22
  53.1 18.6 %collective-permute-start.5 = (f32[8,2,1,64]{2,0,3,1:T(8,128)S(1)}, f32[8,2,1,64]{2,0,3,1:T(8,128)S(1)}, u32[]{:S(2)}, u32[]{:S(2)}) collective-permute-start(f32[8,2,1,64]{2,0,3,1:T(8,128)S(1)} %get-tuple-element.56), channel_id=1, source_target_pairs={{0,16},{16,0},{1,17},{17,1},{2,18},{18,2},{3,19},{19,3},{4,20},{20... | collective-permute-start | bytes 12296 | tf_op jit(solution)/shard_map/ppermute | solution.py:20
  71.9 5.8 %collective-permute-start.6 = (f32[8,2,514,1]{2,0,3,1:T(8,128)S(1)}, f32[8,2,514,1]{2,0,3,1:T(8,128)S(1)}, u32[]{:S(2)}, u32[]{:S(2)}) collective-permute-start(f32[8,2,514,1]{2,0,3,1:T(8,128)S(1)} %get-tuple-element.29), channel_id=1, source_target_pairs={{1,0},{2,1},{3,2},{4,3},{5,4},{6,5},{7,6},{8,7},{9,8},{10,9},{11,1... | collective-permute-start | bytes 98696 | tf_op jit(solution)/shard_map/ppermute | solution.py:22
  76.0 6.3 %collective-permute-start.7 = (f32[8,2,514,1]{2,0,3,1:T(8,128)S(1)}, f32[8,2,514,1]{2,0,3,1:T(8,128)S(1)}, u32[]{:S(2)}, u32[]{:S(2)}) collective-permute-start(f32[8,2,514,1]{2,0,3,1:T(8,128)S(1)} %get-tuple-element.28), channel_id=1, source_target_pairs={{0,1},{1,2},{2,3},{3,4},{4,5},{5,6},{6,7},{7,8},{8,9},{9,10},{10,1... | collective-permute-start | bytes 98696 | tf_op jit(solution)/shard_map/ppermute | solution.py:20
  87.0 14.6 %collective-permute-start.8 = (f32[8,2,1,64]{2,0,3,1:T(8,128)S(1)}, f32[8,2,1,64]{2,0,3,1:T(8,128)S(1)}, u32[]{:S(2)}, u32[]{:S(2)}) collective-permute-start(f32[8,2,1,64]{2,0,3,1:T(8,128)S(1)} %get-tuple-element.53), channel_id=1, source_target_pairs={{16,0},{0,16},{17,1},{1,17},{18,2},{2,18},{19,3},{3,19},{20,4},{4,... | collective-permute-start | bytes 12296 | tf_op jit(solution)/shard_map/ppermute | solution.py:22
  88.6 18.6 %collective-permute-start.9 = (f32[8,2,1,64]{2,0,3,1:T(8,128)S(1)}, f32[8,2,1,64]{2,0,3,1:T(8,128)S(1)}, u32[]{:S(2)}, u32[]{:S(2)}) collective-permute-start(f32[8,2,1,64]{2,0,3,1:T(8,128)S(1)} %get-tuple-element.52), channel_id=1, source_target_pairs={{0,16},{16,0},{1,17},{17,1},{2,18},{18,2},{3,19},{19,3},{4,20},{20... | collective-permute-start | bytes 12296 | tf_op jit(solution)/shard_map/ppermute | solution.py:20
  107.3 4.3 collective-permute-start.10
  110.0 6.1 %collective-permute-start.11 = (f32[8,2,514,1]{2,0,3,1:T(8,128)S(1)}, f32[8,2,514,1]{2,0,3,1:T(8,128)S(1)}, u32[]{:S(2)}, u32[]{:S(2)}) collective-permute-start(f32[8,2,514,1]{2,0,3,1:T(8,128)S(1)} %get-tuple-element.26), channel_id=1, source_target_pairs={{0,1},{1,2},{2,3},{3,4},{4,5},{5,6},{6,7},{7,8},{8,9},{9,10},{10,1... | collective-permute-start | bytes 98696 | tf_op jit(solution)/shard_map/ppermute | solution.py:20
  121.2 14.6 %collective-permute-start.12 = (f32[8,2,1,64]{2,0,3,1:T(8,128)S(1)}, f32[8,2,1,64]{2,0,3,1:T(8,128)S(1)}, u32[]{:S(2)}, u32[]{:S(2)}) collective-permute-start(f32[8,2,1,64]{2,0,3,1:T(8,128)S(1)} %get-tuple-element.49), channel_id=1, source_target_pairs={{16,0},{0,16},{17,1},{1,17},{18,2},{2,18},{19,3},{3,19},{20,4},{4,... | collective-permute-start | bytes 12296 | tf_op jit(solution)/shard_map/ppermute | solution.py:22
  122.8 18.6 %collective-permute-start.13 = (f32[8,2,1,64]{2,0,3,1:T(8,128)S(1)}, f32[8,2,1,64]{2,0,3,1:T(8,128)S(1)}, u32[]{:S(2)}, u32[]{:S(2)}) collective-permute-start(f32[8,2,1,64]{2,0,3,1:T(8,128)S(1)} %get-tuple-element.48), channel_id=1, source_target_pairs={{0,16},{16,0},{1,17},{17,1},{2,18},{18,2},{3,19},{19,3},{4,20},{20... | collective-permute-start | bytes 12296 | tf_op jit(solution)/shard_map/ppermute | solution.py:20
  141.5 3.0 collective-permute-start.14
  142.9 6.3 %collective-permute-start.15 = (f32[8,2,514,1]{2,0,3,1:T(8,128)S(1)}, f32[8,2,514,1]{2,0,3,1:T(8,128)S(1)}, u32[]{:S(2)}, u32[]{:S(2)}) collective-permute-start(f32[8,2,514,1]{2,0,3,1:T(8,128)S(1)} %get-tuple-element.24), channel_id=1, source_target_pairs={{0,1},{1,2},{2,3},{3,4},{4,5},{5,6},{6,7},{7,8},{8,9},{9,10},{10,1... | collective-permute-start | bytes 98696 | tf_op jit(solution)/shard_map/ppermute | solution.py:20
  154.3 95.4 %copy-start.3 = (f32[8,2,512,64]{2,0,3,1:T(8,128)}, f32[8,2,512,64]{2,0,3,1:T(8,128)S(1)}, u32[]{:S(2)}) copy-start(f32[8,2,512,64]{2,0,3,1:T(8,128)S(1)} %fusion.36) | copy-start | bytes 6291460
  154.5 14.6 %collective-permute-start.16 = (f32[8,2,1,64]{2,0,3,1:T(8,128)S(1)}, f32[8,2,1,64]{2,0,3,1:T(8,128)S(1)}, u32[]{:S(2)}, u32[]{:S(2)}) collective-permute-start(f32[8,2,1,64]{2,0,3,1:T(8,128)S(1)} %get-tuple-element.45), channel_id=1, source_target_pairs={{16,0},{0,16},{17,1},{1,17},{18,2},{2,18},{19,3},{3,19},{20,4},{4,... | collective-permute-start | bytes 12296 | tf_op jit(solution)/shard_map/ppermute | solution.py:22
  156.1 18.6 %collective-permute-start.17 = (f32[8,2,1,64]{2,0,3,1:T(8,128)S(1)}, f32[8,2,1,64]{2,0,3,1:T(8,128)S(1)}, u32[]{:S(2)}, u32[]{:S(2)}) collective-permute-start(f32[8,2,1,64]{2,0,3,1:T(8,128)S(1)} %get-tuple-element.44), channel_id=1, source_target_pairs={{0,16},{16,0},{1,17},{17,1},{2,18},{18,2},{3,19},{19,3},{4,20},{20... | collective-permute-start | bytes 12296 | tf_op jit(solution)/shard_map/ppermute | solution.py:20
  174.8 2.6 collective-permute-start.18
  175.8 6.1 %collective-permute-start.19 = (f32[8,2,514,1]{2,0,3,1:T(8,128)S(1)}, f32[8,2,514,1]{2,0,3,1:T(8,128)S(1)}, u32[]{:S(2)}, u32[]{:S(2)}) collective-permute-start(f32[8,2,514,1]{2,0,3,1:T(8,128)S(1)} %get-tuple-element.22), channel_id=1, source_target_pairs={{0,1},{1,2},{2,3},{3,4},{4,5},{5,6},{6,7},{7,8},{8,9},{9,10},{10,1... | collective-permute-start | bytes 98696 | tf_op jit(solution)/shard_map/ppermute | solution.py:20
  187.5 14.6 %collective-permute-start.20 = (f32[8,2,1,64]{2,0,3,1:T(8,128)S(1)}, f32[8,2,1,64]{2,0,3,1:T(8,128)S(1)}, u32[]{:S(2)}, u32[]{:S(2)}) collective-permute-start(f32[8,2,1,64]{2,0,3,1:T(8,128)S(1)} %get-tuple-element.41), channel_id=1, source_target_pairs={{16,0},{0,16},{17,1},{1,17},{18,2},{2,18},{19,3},{3,19},{20,4},{4,... | collective-permute-start | bytes 12296 | tf_op jit(solution)/shard_map/ppermute | solution.py:22
  189.1 18.6 %collective-permute-start.21 = (f32[8,2,1,64]{2,0,3,1:T(8,128)S(1)}, f32[8,2,1,64]{2,0,3,1:T(8,128)S(1)}, u32[]{:S(2)}, u32[]{:S(2)}) collective-permute-start(f32[8,2,1,64]{2,0,3,1:T(8,128)S(1)} %get-tuple-element.40), channel_id=1, source_target_pairs={{0,16},{16,0},{1,17},{17,1},{2,18},{18,2},{3,19},{19,3},{4,20},{20... | collective-permute-start | bytes 12296 | tf_op jit(solution)/shard_map/ppermute | solution.py:20
  207.9 2.8 collective-permute-start.22
  209.0 6.1 %collective-permute-start.23 = (f32[8,2,514,1]{2,0,3,1:T(8,128)S(1)}, f32[8,2,514,1]{2,0,3,1:T(8,128)S(1)}, u32[]{:S(2)}, u32[]{:S(2)}) collective-permute-start(f32[8,2,514,1]{2,0,3,1:T(8,128)S(1)} %get-tuple-element.20), channel_id=1, source_target_pairs={{0,1},{1,2},{2,3},{3,4},{4,5},{5,6},{6,7},{7,8},{8,9},{9,10},{10,1... | collective-permute-start | bytes 98696 | tf_op jit(solution)/shard_map/ppermute | solution.py:20
  220.9 14.6 %collective-permute-start.24 = (f32[8,2,1,64]{2,0,3,1:T(8,128)S(1)}, f32[8,2,1,64]{2,0,3,1:T(8,128)S(1)}, u32[]{:S(2)}, u32[]{:S(2)}) collective-permute-start(f32[8,2,1,64]{2,0,3,1:T(8,128)S(1)} %get-tuple-element.37), channel_id=1, source_target_pairs={{16,0},{0,16},{17,1},{1,17},{18,2},{2,18},{19,3},{3,19},{20,4},{4,... | collective-permute-start | bytes 12296 | tf_op jit(solution)/shard_map/ppermute | solution.py:22
  222.5 18.6 %collective-permute-start.25 = (f32[8,2,1,64]{2,0,3,1:T(8,128)S(1)}, f32[8,2,1,64]{2,0,3,1:T(8,128)S(1)}, u32[]{:S(2)}, u32[]{:S(2)}) collective-permute-start(f32[8,2,1,64]{2,0,3,1:T(8,128)S(1)} %get-tuple-element.36), channel_id=1, source_target_pairs={{0,16},{16,0},{1,17},{17,1},{2,18},{18,2},{3,19},{19,3},{4,20},{20... | collective-permute-start | bytes 12296 | tf_op jit(solution)/shard_map/ppermute | solution.py:20
  241.2 3.6 collective-permute-start.26
  243.2 6.5 %collective-permute-start.27 = (f32[8,2,514,1]{2,0,3,1:T(8,128)S(1)}, f32[8,2,514,1]{2,0,3,1:T(8,128)S(1)}, u32[]{:S(2)}, u32[]{:S(2)}) collective-permute-start(f32[8,2,514,1]{2,0,3,1:T(8,128)S(1)} %get-tuple-element.18), channel_id=1, source_target_pairs={{0,1},{1,2},{2,3},{3,4},{4,5},{5,6},{6,7},{7,8},{8,9},{9,10},{10,1... | collective-permute-start | bytes 98696 | tf_op jit(solution)/shard_map/ppermute | solution.py:20
  255.3 23.6 %copy-start.5 = (f32[8,2,512,64]{2,0,3,1:T(8,128)}, f32[8,2,512,64]{2,0,3,1:T(8,128)S(1)}, u32[]{:S(2)}) copy-start(f32[8,2,512,64]{2,0,3,1:T(8,128)S(1)} %get-tuple-element.76) | copy-start | bytes 6291460
  256.6 14.8 %collective-permute-start.28 = (f32[8,2,1,64]{2,0,3,1:T(8,128)}, f32[8,2,1,64]{2,0,3,1:T(8,128)S(1)}, u32[]{:S(2)}, u32[]{:S(2)}) collective-permute-start(f32[8,2,1,64]{2,0,3,1:T(8,128)} %get-tuple-element.33), channel_id=1, source_target_pairs={{16,0},{0,16},{17,1},{1,17},{18,2},{2,18},{19,3},{3,19},{20,4},{4,... | collective-permute-start | bytes 12296 | tf_op jit(solution)/shard_map/ppermute | solution.py:22
  258.2 18.9 %collective-permute-start.29 = (f32[8,2,1,64]{2,0,3,1:T(8,128)}, f32[8,2,1,64]{2,0,3,1:T(8,128)S(1)}, u32[]{:S(2)}, u32[]{:S(2)}) collective-permute-start(f32[8,2,1,64]{2,0,3,1:T(8,128)} %get-tuple-element.32), channel_id=1, source_target_pairs={{0,16},{16,0},{1,17},{17,1},{2,18},{18,2},{3,19},{19,3},{4,20},{20... | collective-permute-start | bytes 12296 | tf_op jit(solution)/shard_map/ppermute | solution.py:20
  277.0 8.0 %copy-start.12 = (f32[8,2,512,64]{2,0,3,1:T(8,128)S(1)}, f32[8,2,512,64]{2,0,3,1:T(8,128)}, u32[]{:S(2)}) copy-start(f32[8,2,512,64]{2,0,3,1:T(8,128)} %get-tuple-element.75) | copy-start | bytes 6291460
  277.1 3.4 collective-permute-start.30
  278.9 6.1 %copy-start.4 = (f32[8,2,512,64]{2,0,3,1:T(8,128)S(1)}, f32[8,2,512,64]{2,0,3,1:T(8,128)}, u32[]{:S(2)}) copy-start(f32[8,2,512,64]{2,0,3,1:T(8,128)} %copy-done.3) | copy-start | bytes 6291460
  278.9 6.1 %copy-start.11 = (f32[8,2,512,64]{2,0,3,1:T(8,128)S(1)}, f32[8,2,512,64]{2,0,3,1:T(8,128)}, u32[]{:S(2)}) copy-start(f32[8,2,512,64]{2,0,3,1:T(8,128)} %get-tuple-element.73) | copy-start | bytes 6291460
  278.9 6.1 %collective-permute-start.31 = (f32[8,2,514,1]{2,0,3,1:T(8,128)S(1)}, f32[8,2,514,1]{2,0,3,1:T(8,128)S(1)}, u32[]{:S(2)}, u32[]{:S(2)}) collective-permute-start(f32[8,2,514,1]{2,0,3,1:T(8,128)S(1)} %get-tuple-element.16), channel_id=1, source_target_pairs={{0,1},{1,2},{2,3},{3,4},{4,5},{5,6},{6,7},{7,8},{8,9},{9,10},{10,1... | collective-permute-start | bytes 98696 | tf_op jit(solution)/shard_map/ppermute | solution.py:20
  293.8 3.8 copy-start.1
  299.5 71.0 %copy-start.2 = (f32[8,2,512,64]{2,0,3,1:T(8,128)S(1)}, f32[8,2,512,64]{2,0,3,1:T(8,128)}, u32[]{:S(2)}) copy-start(f32[8,2,512,64]{2,0,3,1:T(8,128)} %copy-done.1) | copy-start | bytes 6291460
  299.5 71.0 %all-gather.3.cloned.1.call-start = ((), (), s32[]{:S(2)}) async-start(), calls=%async_computation.3 | async-start | bytes 6291456 | tf_op jit(solution)/shard_map/all_gather | solution.py:64
  300.2 146.8 %all-gather.5.cloned.1.call-start = ((), (), s32[]{:S(2)}) async-start(), calls=%async_computation.5 | async-start | bytes 8912896 | tf_op jit(solution)/shard_map/all_gather | solution.py:77
  314.2 196.8 %reduce-scatter.6.cloned.1.call-start = ((), (), s32[]{:S(2)}) async-start(), calls=%async_computation.4 | async-start | bytes 2228224 | tf_op jit(solution)/shard_map/reduce_scatter | solution.py:70
  380.2 143.6 %reduce-scatter.8.cloned.1.call-start = ((), (), s32[]{:S(2)}) async-start(), calls=%async_computation.6 | async-start | bytes 393216 | tf_op jit(solution)/shard_map/reduce_scatter | solution.py:80
  453.9 58.7 %copy-start.7 = (bf16[1024,128]{1,0:T(8,128)(2,1)S(1)}, bf16[1024,128]{1,0:T(8,128)(2,1)}, u32[]{:S(2)}) copy-start(bf16[1024,128]{1,0:T(8,128)(2,1)} %param.11) | copy-start | bytes 786436
Sparse Core Ops, SparseCore 0:
  299.6 11.9 reduce-scatter.9
  313.8 56.7 all-gather.2
  372.7 74.2 all-gather.4
  450.6 60.3 reduce-scatter.5
  513.1 10.6 reduce-scatter.7
where the time goes:
time: 539 us; the launch traced here: 532 us
  waiting for transfers between devices  387 us (72%)
  matrix products  68 us (13%)
  starting transfers between devices  36.2 us (7%)
  local copies, waits for them, and re-layouts  23 us (4%)
  between operations  14.3 us (3%)
    ppermute x16, waiting for transfers between devices, with_halo(): lax.ppermute(head, axis, [((i + 1) % count, i) for i in range(count)])  111 us
    ppermute x16, waiting for transfers between devices, with_halo(): lax.ppermute(tail, axis, [(i, (i + 1) % count) for i in range(count)])  86 us
    all_gather x1, waiting for transfers between devices, shards(): incoming = lax.all_gather(projected, ('grp', 'gz'), axis=3, tiled=True)  64.2 us
    all_gather x1, waiting for transfers between devices, shards(): lax.all_gather(state, 'sim', axis=2, tiled=True)  56.1 us
    reduce_scatter x1, waiting for transfers between devices, shards(): lax.psum_scatter(gram_rows, ('grp', 'gz'), scatter_dimension=1, tiled=True)  51.4 us
    dot_general x8, matrix products, rates(): jnp.einsum('fg,gzxy->fzxy', coupling, jnp.tanh(center), precision=highest)  45.2 us
    ppermute x16, starting transfers between devices, with_halo(): lax.ppermute(head, axis, [((i + 1) % count, i) for i in range(count)])  31.4 us
    unnamed x6, waiting for transfers between devices  12.1 us
  transfers between devices with their start and end apart: 37, of which 37 were waited for; matrix products, arithmetic and copies ran while one was open for 7% of the time, Pallas kernels for 0%

commit v1 on v0

--- a/solution.py
+++ b/solution.py
@@ -8,6 +8,18 @@
 STEPS = 2
 time_step = 1.0
 highest = lax.Precision.HIGHEST
+
+
+def doubled_up(x, axis, dim):
+    ways, here, lap = (lax.axis_size(axis), lax.axis_index(axis), x.shape[dim])
+    line, have = (x, 1)
+    while have < ways:
+        line = jnp.concatenate(
+            [line, lax.ppermute(line, axis, [(d, (d - have) % ways) for d in range(ways)])],
+            axis=dim,
+        )
+        have = 2 * have
+    return jnp.roll(line, here * lap, axis=dim)
 
 
 def with_halo(cells, sides, width):
@@ -60,9 +72,7 @@
     x_rows = state.shape[2]
     basis_xf = basis_x.astype(jnp.float32)
     basis_yf = basis_y.astype(jnp.float32)
-    block = jnp.einsum(
-        "fzxy,fzwy->xw", state, lax.all_gather(state, "sim", axis=2, tiled=True), precision=highest
-    )
+    block = jnp.einsum("fzxy,fzwy->xw", state, doubled_up(state, "sim", 2), precision=highest)
     gram_rows = block
     own_basis = lax.dynamic_slice_in_dim(basis_xf, lax.axis_index("sim") * x_rows, x_rows, 0)
     partial_proj = jnp.einsum("xr,fzxy->fzry", own_basis, state, precision=highest)

time: 539 us -> 479 us (0.89)
  waiting for transfers between devices: 387 us -> 327 us
    all_gather x1 -> x0, waiting for transfers between devices: 56.1 us -> none  [shards(): lax.all_gather(state, 'sim', axis=2, tiled=True)]
    all_gather x1, waiting for transfers between devices: 64.2 us -> 13.5 us  [shards(): incoming = lax.all_gather(projected, ('grp', 'gz'), axis=3, tiled=True)]
    ppermute x0 -> x1, waiting for transfers between devices: none -> 46.9 us  [doubled_up(): lax.ppermute(line, axis, [(d, (d - have) % ways) for d in range(ways)])]
    unnamed x31 -> x29, local copies, waits for them, and re-layouts: 10.4 us -> 12.1 us
    unnamed x6 -> x5, waiting for transfers between devices: 12.1 us -> 12.2 us
where the time goes in v1:
time: 479 us; the launch traced here: 472 us
  waiting for transfers between devices  327 us (68%)
  matrix products  65 us (14%)
  starting transfers between devices  36.8 us (8%)
  local copies, waits for them, and re-layouts  24.5 us (5%)
  between operations  14.3 us (3%)
    ppermute x16, waiting for transfers between devices, with_halo(): lax.ppermute(head, axis, [((i + 1) % count, i) for i in range(count)])  111 us
    ppermute x16, waiting for transfers between devices, with_halo(): lax.ppermute(tail, axis, [(i, (i + 1) % count) for i in range(count)])  86 us
    reduce_scatter x1, waiting for transfers between devices, shards(): lax.psum_scatter(gram_rows, ('grp', 'gz'), scatter_dimension=1, tiled=True)  51.5 us
    ppermute x1, waiting for transfers between devices, doubled_up(): lax.ppermute(line, axis, [(d, (d - have) % ways) for d in range(ways)])  46.9 us
    dot_general x8, matrix products, rates(): jnp.einsum('fg,gzxy->fzxy', coupling, jnp.tanh(center), precision=highest)  42.2 us
    ppermute x16, starting transfers between devices, with_halo(): lax.ppermute(head, axis, [((i + 1) % count, i) for i in range(count)])  31.4 us
    all_gather x1, waiting for transfers between devices, shards(): incoming = lax.all_gather(projected, ('grp', 'gz'), axis=3, tiled=True)  13.5 us
    unnamed x5, waiting for transfers between devices  12.2 us
  transfers between devices with their start and end apart: 37, of which 37 were waited for; matrix products, arithmetic and copies ran while one was open for 7% of the time, Pallas kernels for 0%

profile of v1, /device:TPU:0, one launch (start us, length us, event | category | flops | bytes accessed | tf_op | source)
XLA Modules:
  0.0 472.4 jit_solution(10738134227841243436)
XLA Ops:
  7.2 2.8 copy.61
  10.3 3.1 collective-permute-start
  13.6 12.5 %collective-permute-done = f32[8,2,1,64]{2,0,3,1:T(8,128)S(1)} collective-permute-done((f32[8,2,1,64]{2,0,3,1:T(8,128)S(1)}, f32[8,2,1,64]{2,0,3,1:T(8,128)S(1)}, u32[]{:S(2)}, u32[]{:S(2)}) %collective-permute-start) | collective-permute-done | bytes 4128 | tf_op jit(solution)/shard_map/ppermute | solution.py:34
  26.1 10.4 %collective-permute-done.1 = f32[8,2,1,64]{2,0,3,1:T(8,128)S(1)} collective-permute-done((f32[8,2,1,64]{2,0,3,1:T(8,128)S(1)}, f32[8,2,1,64]{2,0,3,1:T(8,128)S(1)}, u32[]{:S(2)}, u32[]{:S(2)}) %collective-permute-start.1) | collective-permute-done | bytes 4128 | tf_op jit(solution)/shard_map/ppermute | solution.py:32
  36.6 3.4 collective-permute-start.2
  41.6 4.4 collective-permute-done.3
  46.1 5.3 %multiply_add_fusion.3 = (f32[8,2,512,64]{2,0,3,1:T(8,128)S(1)}, f32[8,2,512,64]{2,0,3,1:T(8,128)S(1)}) fusion(f32[8,2,512,64]{2,3,1,0:T(8,128)S(1)} %copy-done.3, f32[8,2,512,64]{2,3,1,0:T(8,128)S(1)} %tanh.24, f32[8,8]{1,0:T(8,128)S(1)} %copy-done.8, f32[8]{0:T(128)S(1)} %get-tuple-element.65, f32[8]{0:T(128)S(1)} %get-tuple-element.64, ...), kind=kOutput, calls=%fused_computation.171 | convolution fusion | flops 63963136 | bytes 12657248 | tf_op jit(solution)/shard_map/fg,gzxy->fzxy/dot_general | solution.py:53
  51.6 1.6 collective-permute-start.4
  53.7 12.5 %collective-permute-done.4 = f32[8,2,1,64]{2,0,3,1:T(8,128)S(1)} collective-permute-done((f32[8,2,1,64]{2,0,3,1:T(8,128)S(1)}, f32[8,2,1,64]{2,0,3,1:T(8,128)S(1)}, u32[]{:S(2)}, u32[]{:S(2)}) %collective-permute-start.4) | collective-permute-done | bytes 4128 | tf_op jit(solution)/shard_map/ppermute | solution.py:34
  66.2 5.6 %collective-permute-done.5 = f32[8,2,1,64]{2,0,3,1:T(8,128)S(1)} collective-permute-done((f32[8,2,1,64]{2,0,3,1:T(8,128)S(1)}, f32[8,2,1,64]{2,0,3,1:T(8,128)S(1)}, u32[]{:S(2)}, u32[]{:S(2)}) %collective-permute-start.5) | collective-permute-done | bytes 4128 | tf_op jit(solution)/shard_map/ppermute | solution.py:32
  71.9 4.1 collective-permute-start.6
  77.7 4.6 collective-permute-done.7
  82.3 4.5 multiply_add_fusion.2
  87.0 1.6 collective-permute-start.8
  89.1 12.5 %collective-permute-done.8 = f32[8,2,1,64]{2,0,3,1:T(8,128)S(1)} collective-permute-done((f32[8,2,1,64]{2,0,3,1:T(8,128)S(1)}, f32[8,2,1,64]{2,0,3,1:T(8,128)S(1)}, u32[]{:S(2)}, u32[]{:S(2)}) %collective-permute-start.8) | collective-permute-done | bytes 4128 | tf_op jit(solution)/shard_map/ppermute | solution.py:34
  101.6 5.6 %collective-permute-done.9 = f32[8,2,1,64]{2,0,3,1:T(8,128)S(1)} collective-permute-done((f32[8,2,1,64]{2,0,3,1:T(8,128)S(1)}, f32[8,2,1,64]{2,0,3,1:T(8,128)S(1)}, u32[]{:S(2)}, u32[]{:S(2)}) %collective-permute-start.9) | collective-permute-done | bytes 4128 | tf_op jit(solution)/shard_map/ppermute | solution.py:32
  107.4 2.7 collective-permute-start.10
  110.2 1.5 collective-permute-done.10
  111.7 4.4 collective-permute-done.11
  116.1 4.9 %copy_add_fusion = (f32[8,2,512,64]{2,0,3,1:T(8,128)S(1)}, f32[8,2,512,64]{2,0,3,1:T(8,128)S(1)}) fusion(f32[8,2,512,64]{2,3,1,0:T(8,128)S(1)} %copy-done.3, f32[8,8]{1,0:T(8,128)S(1)} %copy-done.8, f32[8,2,512,64]{2,0,3,1:T(8,128)S(1)} %get-tuple-element.68, f32[8]{0:T(128)S(1)} %get-tuple-element.65, f32[8]{0:T(128)S(1)} %get-tuple-element.64, ...), kind=kOutput, calls=%fused_computation.219 | convolution fusion | flops 63438848 | bytes 10560096 | tf_op jit(solution)/shard_map/fg,gzxy->fzxy/dot_general | solution.py:53
  121.2 1.6 collective-permute-start.12
  123.3 12.5 %collective-permute-done.12 = f32[8,2,1,64]{2,0,3,1:T(8,128)S(1)} collective-permute-done((f32[8,2,1,64]{2,0,3,1:T(8,128)S(1)}, f32[8,2,1,64]{2,0,3,1:T(8,128)S(1)}, u32[]{:S(2)}, u32[]{:S(2)}) %collective-permute-start.12) | collective-permute-done | bytes 4128 | tf_op jit(solution)/shard_map/ppermute | solution.py:34
  135.8 5.6 %collective-permute-done.13 = f32[8,2,1,64]{2,0,3,1:T(8,128)S(1)} collective-permute-done((f32[8,2,1,64]{2,0,3,1:T(8,128)S(1)}, f32[8,2,1,64]{2,0,3,1:T(8,128)S(1)}, u32[]{:S(2)}, u32[]{:S(2)}) %collective-permute-start.13) | collective-permute-done | bytes 4128 | tf_op jit(solution)/shard_map/ppermute | solution.py:32
  144.5 4.6 collective-permute-done.15
  149.2 5.1 %fusion.39 = f32[8,2,512,64]{2,0,3,1:T(8,128)S(1)} fusion(f32[8,1,512,64]{2,0,3,1:T(8,128)S(1)} %get-tuple-element.51, f32[8,1,512,64]{2,0,3,1:T(8,128)S(1)} %get-tuple-element.50, f32[8,2,514,1]{2,0,3,1:T(8,128)S(1)} %collective-permute-done.14, f32[8,2,1,64]{2,0,3,1:T(8,128)S(1)} %collective-permute-done.12, f32[8,2,512,64]{2,0,3,1:T(8,128)S(1)} %get-tuple-element.70, ...), kind=kOutput, calls=%fused_computation.51 | convolution fusion | flops 66584576 | bytes 14754400 | tf_op jit(solution)/shard_map/fg,gzxy->fzxy/dot_general | solution.py:53
  154.5 1.6 collective-permute-start.16
  156.6 12.5 %collective-permute-done.16 = f32[8,2,1,64]{2,0,3,1:T(8,128)S(1)} collective-permute-done((f32[8,2,1,64]{2,0,3,1:T(8,128)S(1)}, f32[8,2,1,64]{2,0,3,1:T(8,128)S(1)}, u32[]{:S(2)}, u32[]{:S(2)}) %collective-permute-start.16) | collective-permute-done | bytes 4128 | tf_op jit(solution)/shard_map/ppermute | solution.py:34
  169.1 5.6 %collective-permute-done.17 = f32[8,2,1,64]{2,0,3,1:T(8,128)S(1)} collective-permute-done((f32[8,2,1,64]{2,0,3,1:T(8,128)S(1)}, f32[8,2,1,64]{2,0,3,1:T(8,128)S(1)}, u32[]{:S(2)}, u32[]{:S(2)}) %collective-permute-start.17) | collective-permute-done | bytes 4128 | tf_op jit(solution)/shard_map/ppermute | solution.py:32
  176.0 1.5 collective-permute-done.18
  177.5 4.4 collective-permute-done.19
  181.9 5.3 %multiply_add_fusion.1 = (f32[8,2,512,64]{2,0,3,1:T(8,128)S(1)}, f32[8,2,512,64]{2,0,3,1:T(8,128)}) fusion(f32[8,2,512,64]{2,0,3,1:T(8,128)S(1)} %fusion.39, f32[8,8]{1,0:T(8,128)S(1)} %copy-done.8, f32[8]{0:T(128)S(1)} %get-tuple-element.65, f32[8]{0:T(128)S(1)} %get-tuple-element.64, f32[8,2,1,64]{2,0,3,1:T(8,128)S(1)} %collective-permute-done.16, ...), kind=kOutput, calls=%fused_computation.161 | convolution fusion | flops 63963136 | bytes 8462944 | tf_op jit(solution)/shard_map/fg,gzxy->fzxy/dot_general | solution.py:53
  187.5 1.6 collective-permute-start.20
  189.6 12.5 %collective-permute-done.20 = f32[8,2,1,64]{2,0,3,1:T(8,128)S(1)} collective-permute-done((f32[8,2,1,64]{2,0,3,1:T(8,128)S(1)}, f32[8,2,1,64]{2,0,3,1:T(8,128)S(1)}, u32[]{:S(2)}, u32[]{:S(2)}) %collective-permute-start.20) | collective-permute-done | bytes 4128 | tf_op jit(solution)/shard_map/ppermute | solution.py:34
  202.1 5.6 %collective-permute-done.21 = f32[8,2,1,64]{2,0,3,1:T(8,128)S(1)} collective-permute-done((f32[8,2,1,64]{2,0,3,1:T(8,128)S(1)}, f32[8,2,1,64]{2,0,3,1:T(8,128)S(1)}, u32[]{:S(2)}, u32[]{:S(2)}) %collective-permute-start.21) | collective-permute-done | bytes 4128 | tf_op jit(solution)/shard_map/ppermute | solution.py:32
  209.1 1.5 collective-permute-done.22
  210.6 4.4 collective-permute-done.23
  215.1 5.6 %multiply_add_fusion = (f32[8,2,512,64]{2,0,3,1:T(8,128)S(1)}, f32[8,2,512,64]{2,0,3,1:T(8,128)}) fusion(f32[8,2,512,64]{2,0,3,1:T(8,128)S(1)} %fusion.39, f32[8,8]{1,0:T(8,128)S(1)} %copy-done.8, f32[8,2,512,64]{2,0,3,1:T(8,128)S(1)} %get-tuple-element.72, f32[8]{0:T(128)S(1)} %get-tuple-element.65, f32[8]{0:T(128)S(1)} %get-tuple-element.64, ...), kind=kOutput, calls=%fused_computation.158 | convolution fusion | flops 63963136 | bytes 10560096 | tf_op jit(solution)/shard_map/fg,gzxy->fzxy/dot_general | solution.py:53
  220.9 1.6 collective-permute-start.24
  223.0 12.5 %collective-permute-done.24 = f32[8,2,1,64]{2,0,3,1:T(8,128)S(1)} collective-permute-done((f32[8,2,1,64]{2,0,3,1:T(8,128)S(1)}, f32[8,2,1,64]{2,0,3,1:T(8,128)S(1)}, u32[]{:S(2)}, u32[]{:S(2)}) %collective-permute-start.24) | collective-permute-done | bytes 4128 | tf_op jit(solution)/shard_map/ppermute | solution.py:34
  235.5 5.6 %collective-permute-done.25 = f32[8,2,1,64]{2,0,3,1:T(8,128)S(1)} collective-permute-done((f32[8,2,1,64]{2,0,3,1:T(8,128)S(1)}, f32[8,2,1,64]{2,0,3,1:T(8,128)S(1)}, u32[]{:S(2)}, u32[]{:S(2)}) %collective-permute-start.25) | collective-permute-done | bytes 4128 | tf_op jit(solution)/shard_map/ppermute | solution.py:32
  241.2 1.9 collective-permute-start.26
  244.8 4.8 %collective-permute-done.27 = f32[8,2,514,1]{2,0,3,1:T(8,128)S(1)} collective-permute-done((f32[8,2,514,1]{2,0,3,1:T(8,128)S(1)}, f32[8,2,514,1]{2,0,3,1:T(8,128)S(1)}, u32[]{:S(2)}, u32[]{:S(2)}) %collective-permute-start.27) | collective-permute-done | bytes 32928 | tf_op jit(solution)/shard_map/ppermute | solution.py:32
  249.7 5.6 %fusion.161 = (f32[8,2,512,64]{2,0,3,1:T(8,128)S(1)}, f32[8,2,512,64]{2,0,3,1:T(8,128)}) fusion(f32[8,2,512,64]{2,0,3,1:T(8,128)S(1)} %fusion.39, f32[8,8]{1,0:T(8,128)S(1)} %copy-done.8, f32[8,2,512,64]{2,0,3,1:T(8,128)S(1)} %get-tuple-element.74, f32[8]{0:T(128)S(1)} %get-tuple-element.65, f32[8]{0:T(128)S(1)} %get-tuple-element.64, ...), kind=kOutput, calls=%fused_computation.236 | convolution fusion | flops 63438848 | bytes 10560096 | tf_op jit(solution)/shard_map/fg,gzxy->fzxy/dot_general | solution.py:53
  255.2 1.4 copy-done.1
  257.8 1.5 collective-permute-start.28
  259.8 12.7 %collective-permute-done.28 = f32[8,2,1,64]{2,0,3,1:T(8,128)S(1)} collective-permute-done((f32[8,2,1,64]{2,0,3,1:T(8,128)}, f32[8,2,1,64]{2,0,3,1:T(8,128)S(1)}, u32[]{:S(2)}, u32[]{:S(2)}) %collective-permute-start.28) | collective-permute-done | bytes 4128 | tf_op jit(solution)/shard_map/ppermute | solution.py:34
  272.5 5.6 %collective-permute-done.29 = f32[8,2,1,64]{2,0,3,1:T(8,128)S(1)} collective-permute-done((f32[8,2,1,64]{2,0,3,1:T(8,128)}, f32[8,2,1,64]{2,0,3,1:T(8,128)S(1)}, u32[]{:S(2)}, u32[]{:S(2)}) %collective-permute-start.29) | collective-permute-done | bytes 4128 | tf_op jit(solution)/shard_map/ppermute | solution.py:32
  279.0 1.8 collective-permute-start.30
  281.0 1.5 collective-permute-done.30
  282.4 4.5 collective-permute-done.31
  286.9 5.9 %fusion.74 = f32[8,2,512,64]{2,0,3,1:T(8,128)S(1)} fusion(f32[8,2,512,64]{2,0,3,1:T(8,128)S(1)} %fusion.39, f32[8,1,512,64]{2,0,3,1:T(8,128)S(1)} %get-tuple-element.35, f32[8,1,512,64]{2,0,3,1:T(8,128)S(1)} %get-tuple-element.34, f32[8,2,514,1]{2,0,3,1:T(8,128)S(1)} %collective-permute-done.30, f32[8,2,1,64]{2,0,3,1:T(8,128)S(1)} %collective-permute-done.28, ...), kind=kOutput, calls=%fused_computation.86 | convolution fusion | flops 66584576 | bytes 14754400 | tf_op jit(solution)/shard_map/fg,gzxy->fzxy/dot_general | solution.py:53
  296.1 1.8 reshape.20
  298.0 12.1 %reduce-scatter.10.cloned.1.call-done = f32[64,1024]{1,0:T(8,128)} async-done(((f32[128,1024]{1,0:T(8,128)}), f32[64,1024]{1,0:T(8,128)}) %reduce-scatter.10.cloned.1.call-update) | async-done | bytes 262160
  313.3 46.9 %collective-permute-done.32 = f32[8,2,512,64]{2,0,3,1:T(8,128)} collective-permute-done((f32[8,2,512,64]{2,0,3,1:T(8,128)S(1)}, f32[8,2,512,64]{2,0,3,1:T(8,128)}, u32[]{:S(2)}, u32[]{:S(2)}) %collective-permute-start.32) | collective-permute-done | bytes 2097184 | tf_op jit(solution)/shard_map/ppermute | solution.py:18
  360.2 10.5 %fusion.92 = f32[512,1024]{0,1:T(8,128)} fusion(f32[8,2,512,64]{2,0,3,1:T(8,128)S(1)} %copy-done.5, s32[]{:T(128)S(6)} %select_n.20, f32[8,2,512,64]{2,0,3,1:T(8,128)} %collective-permute-done.32), kind=kOutput, calls=%fused_computation.172 | convolution fusion | flops 6445596672 | bytes 8388612 | tf_op jit(solution)/shard_map/fzxy,fzwy->xw/dot_general | solution.py:75
  371.0 2.5 copy.69
  373.5 13.5 %all-gather.2.cloned.1.call-done = f32[8,2,64,1024]{2,0,1,3:T(8,128)} async-done(((f32[8,2,64,64]{2,0,1,3:T(8,128)}), f32[8,2,64,1024]{2,0,1,3:T(8,128)}) %all-gather.2.cloned.1.call-update) | async-done | bytes 4194320 | tf_op jit(solution)/shard_map/all_gather | solution.py:87
  387.1 6.9 %copy.66 = f32[8,2,64,1024]{3,2,1,0:T(8,128)} copy(f32[8,2,64,1024]{2,0,1,3:T(8,128)} %all-gather.2.cloned.1.call-done) | data formatting | bytes 8388608 | tf_op jit(solution)/shard_map/all_gather | solution.py:87
  394.0 5.8 %convolution_bitcast_fusion.1 = f32[64,1024]{1,0:T(8,128)} fusion(f32[8,2,64,1024]{3,2,1,0:T(8,128)} %copy.66, f32[8,2,64,64]{3,1,0,2:T(2,128)S(1)} %bitcast.93), kind=kOutput, calls=%fused_computation.174 | convolution fusion | flops 805306368 | bytes 4718592 | tf_op jit(solution)/shard_map/fzry,fzrv->yv/dot_general | solution.py:88
  399.8 51.5 %reduce-scatter.6.cloned.1.call-done = f32[512,64]{0,1:T(8,128)} async-done(((f32[512,1024]{0,1:T(8,128)}), f32[512,64]{0,1:T(8,128)}) %reduce-scatter.6.cloned.1.call-update) | async-done | bytes 131088 | tf_op jit(solution)/shard_map/reduce_scatter | solution.py:80
  451.3 1.6 broadcast_multiply_fusion.1
  452.8 5.5 %fusion.98 = f32[8,2,64,8]{2,3,1,0:T(8,128)} fusion(f32[8,2,64,1024]{3,2,1,0:T(8,128)} %copy.66, bf16[1024,128]{1,0:T(8,128)(2,1)S(1)} %copy-done.6, s32[]{:T(128)S(6)} %select_n.22), kind=kOutput, calls=%fused_computation.176 | convolution fusion | flops 100663296 | bytes 4489220 | tf_op jit(solution)/shard_map/vs,fzrv->fzrs/dot_general | solution.py:89
  458.3 5.8 %reduce-scatter.8.cloned.1.call-done = f32[64,512]{1,0:T(8,128)} async-done(((f32[64,1024]{1,0:T(8,128)}), f32[64,512]{1,0:T(8,128)}) %reduce-scatter.8.cloned.1.call-update) | async-done | bytes 131088 | tf_op jit(solution)/shard_map/reduce_scatter | solution.py:90
  464.1 1.6 broadcast_multiply_fusion
  (85 shorter events, 25.5 us)
Async XLA Ops:
  7.2 287.0 %copy-start = (bf16[1024,128]{1,0:T(8,128)(2,1)S(1)}, bf16[1024,128]{1,0:T(8,128)(2,1)}, u32[]{:S(2)}) copy-start(bf16[1024,128]{1,0:T(8,128)(2,1)} %param.10) | copy-start | bytes 786436
  7.2 302.9 %reduce-scatter.10.cloned.1.call-start = ((), (), s32[]{:S(2)}) async-start(), calls=%async_computation.6 | async-start | bytes 786432
  10.3 15.8 %collective-permute-start = (f32[8,2,1,64]{2,0,3,1:T(8,128)S(1)}, f32[8,2,1,64]{2,0,3,1:T(8,128)S(1)}, u32[]{:S(2)}, u32[]{:S(2)}) collective-permute-start(f32[8,2,1,64]{2,0,3,1:T(8,128)S(1)} %get-tuple-element.61), channel_id=1, source_target_pairs={{16,0},{0,16},{17,1},{1,17},{18,2},{2,18},{19,3},{3,19},{20,4},{4,... | collective-permute-start | bytes 12296 | tf_op jit(solution)/shard_map/ppermute | solution.py:34
  13.3 23.2 %collective-permute-start.1 = (f32[8,2,1,64]{2,0,3,1:T(8,128)S(1)}, f32[8,2,1,64]{2,0,3,1:T(8,128)S(1)}, u32[]{:S(2)}, u32[]{:S(2)}) collective-permute-start(f32[8,2,1,64]{2,0,3,1:T(8,128)S(1)} %get-tuple-element.60), channel_id=1, source_target_pairs={{0,16},{16,0},{1,17},{17,1},{2,18},{18,2},{3,19},{19,3},{4,20},{20... | collective-permute-start | bytes 12296 | tf_op jit(solution)/shard_map/ppermute | solution.py:32
  13.6 26.4 %copy-start.7 = (f32[2,8]{1,0:T(2,128)S(1)}, f32[2,8]{1,0:T(2,128)}, u32[]{:S(2)}) copy-start(f32[2,8]{1,0:T(2,128)} %param.8) | copy-start | bytes 196
  13.6 26.4 %copy-start.3 = (f32[8,2,512,64]{2,3,1,0:T(8,128)S(1)}, f32[8,2,512,64]{2,3,1,0:T(8,128)}, u32[]{:S(2)}) copy-start(f32[8,2,512,64]{2,3,1,0:T(8,128)} %param.6) | copy-start | bytes 6291460
  36.6 5.1 %collective-permute-start.2 = (f32[8,2,514,1]{2,0,3,1:T(8,128)S(1)}, f32[8,2,514,1]{2,0,3,1:T(8,128)S(1)}, u32[]{:S(2)}, u32[]{:S(2)}) collective-permute-start(f32[8,2,514,1]{2,0,3,1:T(8,128)S(1)} %get-tuple-element.31), channel_id=1, source_target_pairs={{1,0},{2,1},{3,2},{4,3},{5,4},{6,5},{7,6},{8,7},{9,8},{10,9},{11,1... | collective-permute-start | bytes 98696 | tf_op jit(solution)/shard_map/ppermute | solution.py:34
  40.0 6.1 %collective-permute-start.3 = (f32[8,2,514,1]{2,0,3,1:T(8,128)S(1)}, f32[8,2,514,1]{2,0,3,1:T(8,128)S(1)}, u32[]{:S(2)}, u32[]{:S(2)}) collective-permute-start(f32[8,2,514,1]{2,0,3,1:T(8,128)S(1)} %get-tuple-element.30), channel_id=1, source_target_pairs={{0,1},{1,2},{2,3},{3,4},{4,5},{5,6},{6,7},{7,8},{8,9},{9,10},{10,1... | collective-permute-start | bytes 98696 | tf_op jit(solution)/shard_map/ppermute | solution.py:32
  40.0 6.1 %copy-start.8 = (f32[8,8]{1,0:T(8,128)S(1)}, f32[8,8]{1,0:T(8,128)}, u32[]{:S(2)}) copy-start(f32[8,8]{1,0:T(8,128)} %param.9) | copy-start | bytes 772
  40.0 6.1 %copy-start.9 = (f32[8]{0:T(128)S(1)}, f32[8]{0:T(128)}, u32[]{:S(2)}) copy-start(f32[8]{0:T(128)} %param.7) | copy-start | bytes 100
  51.6 14.6 %collective-permute-start.4 = (f32[8,2,1,64]{2,0,3,1:T(8,128)S(1)}, f32[8,2,1,64]{2,0,3,1:T(8,128)S(1)}, u32[]{:S(2)}, u32[]{:S(2)}) collective-permute-start(f32[8,2,1,64]{2,0,3,1:T(8,128)S(1)} %get-tuple-element.57), channel_id=1, source_target_pairs={{16,0},{0,16},{17,1},{1,17},{18,2},{2,18},{19,3},{3,19},{20,4},{4,... | collective-permute-start | bytes 12296 | tf_op jit(solution)/shard_map/ppermute | solution.py:34
  53.1 18.6 %collective-permute-start.5 = (f32[8,2,1,64]{2,0,3,1:T(8,128)S(1)}, f32[8,2,1,64]{2,0,3,1:T(8,128)S(1)}, u32[]{:S(2)}, u32[]{:S(2)}) collective-permute-start(f32[8,2,1,64]{2,0,3,1:T(8,128)S(1)} %get-tuple-element.56), channel_id=1, source_target_pairs={{0,16},{16,0},{1,17},{17,1},{2,18},{18,2},{3,19},{19,3},{4,20},{20... | collective-permute-start | bytes 12296 | tf_op jit(solution)/shard_map/ppermute | solution.py:32
  71.9 5.8 %collective-permute-start.6 = (f32[8,2,514,1]{2,0,3,1:T(8,128)S(1)}, f32[8,2,514,1]{2,0,3,1:T(8,128)S(1)}, u32[]{:S(2)}, u32[]{:S(2)}) collective-permute-start(f32[8,2,514,1]{2,0,3,1:T(8,128)S(1)} %get-tuple-element.29), channel_id=1, source_target_pairs={{1,0},{2,1},{3,2},{4,3},{5,4},{6,5},{7,6},{8,7},{9,8},{10,9},{11,1... | collective-permute-start | bytes 98696 | tf_op jit(solution)/shard_map/ppermute | solution.py:34
  76.0 6.3 %collective-permute-start.7 = (f32[8,2,514,1]{2,0,3,1:T(8,128)S(1)}, f32[8,2,514,1]{2,0,3,1:T(8,128)S(1)}, u32[]{:S(2)}, u32[]{:S(2)}) collective-permute-start(f32[8,2,514,1]{2,0,3,1:T(8,128)S(1)} %get-tuple-element.28), channel_id=1, source_target_pairs={{0,1},{1,2},{2,3},{3,4},{4,5},{5,6},{6,7},{7,8},{8,9},{9,10},{10,1... | collective-permute-start | bytes 98696 | tf_op jit(solution)/shard_map/ppermute | solution.py:32
  87.0 14.6 %collective-permute-start.8 = (f32[8,2,1,64]{2,0,3,1:T(8,128)S(1)}, f32[8,2,1,64]{2,0,3,1:T(8,128)S(1)}, u32[]{:S(2)}, u32[]{:S(2)}) collective-permute-start(f32[8,2,1,64]{2,0,3,1:T(8,128)S(1)} %get-tuple-element.53), channel_id=1, source_target_pairs={{16,0},{0,16},{17,1},{1,17},{18,2},{2,18},{19,3},{3,19},{20,4},{4,... | collective-permute-start | bytes 12296 | tf_op jit(solution)/shard_map/ppermute | solution.py:34
  88.6 18.6 %collective-permute-start.9 = (f32[8,2,1,64]{2,0,3,1:T(8,128)S(1)}, f32[8,2,1,64]{2,0,3,1:T(8,128)S(1)}, u32[]{:S(2)}, u32[]{:S(2)}) collective-permute-start(f32[8,2,1,64]{2,0,3,1:T(8,128)S(1)} %get-tuple-element.52), channel_id=1, source_target_pairs={{0,16},{16,0},{1,17},{17,1},{2,18},{18,2},{3,19},{19,3},{4,20},{20... | collective-permute-start | bytes 12296 | tf_op jit(solution)/shard_map/ppermute | solution.py:32
  107.4 4.3 collective-permute-start.10
  110.0 6.1 %collective-permute-start.11 = (f32[8,2,514,1]{2,0,3,1:T(8,128)S(1)}, f32[8,2,514,1]{2,0,3,1:T(8,128)S(1)}, u32[]{:S(2)}, u32[]{:S(2)}) collective-permute-start(f32[8,2,514,1]{2,0,3,1:T(8,128)S(1)} %get-tuple-element.26), channel_id=1, source_target_pairs={{0,1},{1,2},{2,3},{3,4},{4,5},{5,6},{6,7},{7,8},{8,9},{9,10},{10,1... | collective-permute-start | bytes 98696 | tf_op jit(solution)/shard_map/ppermute | solution.py:32
  121.2 14.6 %collective-permute-start.12 = (f32[8,2,1,64]{2,0,3,1:T(8,128)S(1)}, f32[8,2,1,64]{2,0,3,1:T(8,128)S(1)}, u32[]{:S(2)}, u32[]{:S(2)}) collective-permute-start(f32[8,2,1,64]{2,0,3,1:T(8,128)S(1)} %get-tuple-element.49), channel_id=1, source_target_pairs={{16,0},{0,16},{17,1},{1,17},{18,2},{2,18},{19,3},{3,19},{20,4},{4,... | collective-permute-start | bytes 12296 | tf_op jit(solution)/shard_map/ppermute | solution.py:34
  122.8 18.6 %collective-permute-start.13 = (f32[8,2,1,64]{2,0,3,1:T(8,128)S(1)}, f32[8,2,1,64]{2,0,3,1:T(8,128)S(1)}, u32[]{:S(2)}, u32[]{:S(2)}) collective-permute-start(f32[8,2,1,64]{2,0,3,1:T(8,128)S(1)} %get-tuple-element.48), channel_id=1, source_target_pairs={{0,16},{16,0},{1,17},{17,1},{2,18},{18,2},{3,19},{19,3},{4,20},{20... | collective-permute-start | bytes 12296 | tf_op jit(solution)/shard_map/ppermute | solution.py:32
  141.5 3.0 collective-permute-start.14
  142.9 6.3 %collective-permute-start.15 = (f32[8,2,514,1]{2,0,3,1:T(8,128)S(1)}, f32[8,2,514,1]{2,0,3,1:T(8,128)S(1)}, u32[]{:S(2)}, u32[]{:S(2)}) collective-permute-start(f32[8,2,514,1]{2,0,3,1:T(8,128)S(1)} %get-tuple-element.24), channel_id=1, source_target_pairs={{0,1},{1,2},{2,3},{3,4},{4,5},{5,6},{6,7},{7,8},{8,9},{9,10},{10,1... | collective-permute-start | bytes 98696 | tf_op jit(solution)/shard_map/ppermute | solution.py:32
  154.5 14.6 %collective-permute-start.16 = (f32[8,2,1,64]{2,0,3,1:T(8,128)S(1)}, f32[8,2,1,64]{2,0,3,1:T(8,128)S(1)}, u32[]{:S(2)}, u32[]{:S(2)}) collective-permute-start(f32[8,2,1,64]{2,0,3,1:T(8,128)S(1)} %get-tuple-element.45), channel_id=1, source_target_pairs={{16,0},{0,16},{17,1},{1,17},{18,2},{2,18},{19,3},{3,19},{20,4},{4,... | collective-permute-start | bytes 12296 | tf_op jit(solution)/shard_map/ppermute | solution.py:34
  156.1 18.6 %collective-permute-start.17 = (f32[8,2,1,64]{2,0,3,1:T(8,128)S(1)}, f32[8,2,1,64]{2,0,3,1:T(8,128)S(1)}, u32[]{:S(2)}, u32[]{:S(2)}) collective-permute-start(f32[8,2,1,64]{2,0,3,1:T(8,128)S(1)} %get-tuple-element.44), channel_id=1, source_target_pairs={{0,16},{16,0},{1,17},{17,1},{2,18},{18,2},{3,19},{19,3},{4,20},{20... | collective-permute-start | bytes 12296 | tf_op jit(solution)/shard_map/ppermute | solution.py:32
  174.8 2.6 collective-permute-start.18
  175.8 6.1 %collective-permute-start.19 = (f32[8,2,514,1]{2,0,3,1:T(8,128)S(1)}, f32[8,2,514,1]{2,0,3,1:T(8,128)S(1)}, u32[]{:S(2)}, u32[]{:S(2)}) collective-permute-start(f32[8,2,514,1]{2,0,3,1:T(8,128)S(1)} %get-tuple-element.22), channel_id=1, source_target_pairs={{0,1},{1,2},{2,3},{3,4},{4,5},{5,6},{6,7},{7,8},{8,9},{9,10},{10,1... | collective-permute-start | bytes 98696 | tf_op jit(solution)/shard_map/ppermute | solution.py:32
  187.5 14.6 %collective-permute-start.20 = (f32[8,2,1,64]{2,0,3,1:T(8,128)S(1)}, f32[8,2,1,64]{2,0,3,1:T(8,128)S(1)}, u32[]{:S(2)}, u32[]{:S(2)}) collective-permute-start(f32[8,2,1,64]{2,0,3,1:T(8,128)S(1)} %get-tuple-element.41), channel_id=1, source_target_pairs={{16,0},{0,16},{17,1},{1,17},{18,2},{2,18},{19,3},{3,19},{20,4},{4,... | collective-permute-start | bytes 12296 | tf_op jit(solution)/shard_map/ppermute | solution.py:34
  189.1 18.6 %collective-permute-start.21 = (f32[8,2,1,64]{2,0,3,1:T(8,128)S(1)}, f32[8,2,1,64]{2,0,3,1:T(8,128)S(1)}, u32[]{:S(2)}, u32[]{:S(2)}) collective-permute-start(f32[8,2,1,64]{2,0,3,1:T(8,128)S(1)} %get-tuple-element.40), channel_id=1, source_target_pairs={{0,16},{16,0},{1,17},{17,1},{2,18},{18,2},{3,19},{19,3},{4,20},{20... | collective-permute-start | bytes 12296 | tf_op jit(solution)/shard_map/ppermute | solution.py:32
  207.8 2.8 collective-permute-start.22
  209.0 6.1 %collective-permute-start.23 = (f32[8,2,514,1]{2,0,3,1:T(8,128)S(1)}, f32[8,2,514,1]{2,0,3,1:T(8,128)S(1)}, u32[]{:S(2)}, u32[]{:S(2)}) collective-permute-start(f32[8,2,514,1]{2,0,3,1:T(8,128)S(1)} %get-tuple-element.20), channel_id=1, source_target_pairs={{0,1},{1,2},{2,3},{3,4},{4,5},{5,6},{6,7},{7,8},{8,9},{9,10},{10,1... | collective-permute-start | bytes 98696 | tf_op jit(solution)/shard_map/ppermute | solution.py:32
  220.9 14.6 %collective-permute-start.24 = (f32[8,2,1,64]{2,0,3,1:T(8,128)S(1)}, f32[8,2,1,64]{2,0,3,1:T(8,128)S(1)}, u32[]{:S(2)}, u32[]{:S(2)}) collective-permute-start(f32[8,2,1,64]{2,0,3,1:T(8,128)S(1)} %get-tuple-element.37), channel_id=1, source_target_pairs={{16,0},{0,16},{17,1},{1,17},{18,2},{2,18},{19,3},{3,19},{20,4},{4,... | collective-permute-start | bytes 12296 | tf_op jit(solution)/shard_map/ppermute | solution.py:34
  222.5 18.6 %collective-permute-start.25 = (f32[8,2,1,64]{2,0,3,1:T(8,128)S(1)}, f32[8,2,1,64]{2,0,3,1:T(8,128)S(1)}, u32[]{:S(2)}, u32[]{:S(2)}) collective-permute-start(f32[8,2,1,64]{2,0,3,1:T(8,128)S(1)} %get-tuple-element.36), channel_id=1, source_target_pairs={{0,16},{16,0},{1,17},{17,1},{2,18},{18,2},{3,19},{19,3},{4,20},{20... | collective-permute-start | bytes 12296 | tf_op jit(solution)/shard_map/ppermute | solution.py:32
  241.2 3.6 collective-permute-start.26
  243.1 6.5 %collective-permute-start.27 = (f32[8,2,514,1]{2,0,3,1:T(8,128)S(1)}, f32[8,2,514,1]{2,0,3,1:T(8,128)S(1)}, u32[]{:S(2)}, u32[]{:S(2)}) collective-permute-start(f32[8,2,514,1]{2,0,3,1:T(8,128)S(1)} %get-tuple-element.18), channel_id=1, source_target_pairs={{0,1},{1,2},{2,3},{3,4},{4,5},{5,6},{6,7},{7,8},{8,9},{9,10},{10,1... | collective-permute-start | bytes 98696 | tf_op jit(solution)/shard_map/ppermute | solution.py:32
  255.2 1.4 copy-start.1
  257.8 14.8 %collective-permute-start.28 = (f32[8,2,1,64]{2,0,3,1:T(8,128)}, f32[8,2,1,64]{2,0,3,1:T(8,128)S(1)}, u32[]{:S(2)}, u32[]{:S(2)}) collective-permute-start(f32[8,2,1,64]{2,0,3,1:T(8,128)} %get-tuple-element.33), channel_id=1, source_target_pairs={{16,0},{0,16},{17,1},{1,17},{18,2},{2,18},{19,3},{3,19},{20,4},{4,... | collective-permute-start | bytes 12296 | tf_op jit(solution)/shard_map/ppermute | solution.py:34
  259.3 18.8 %collective-permute-start.29 = (f32[8,2,1,64]{2,0,3,1:T(8,128)}, f32[8,2,1,64]{2,0,3,1:T(8,128)S(1)}, u32[]{:S(2)}, u32[]{:S(2)}) collective-permute-start(f32[8,2,1,64]{2,0,3,1:T(8,128)} %get-tuple-element.32), channel_id=1, source_target_pairs={{0,16},{16,0},{1,17},{17,1},{2,18},{18,2},{3,19},{19,3},{4,20},{20... | collective-permute-start | bytes 12296 | tf_op jit(solution)/shard_map/ppermute | solution.py:32
  259.8 21.0 %copy-start.2 = (f32[8,2,512,64]{2,0,3,1:T(8,128)S(1)}, f32[8,2,512,64]{2,0,3,1:T(8,128)}, u32[]{:S(2)}) copy-start(f32[8,2,512,64]{2,0,3,1:T(8,128)} %copy-done.1) | copy-start | bytes 6291460
  279.0 3.4 collective-permute-start.30
  280.8 6.1 %copy-start.10 = (f32[8,2,512,64]{2,0,3,1:T(8,128)S(1)}, f32[8,2,512,64]{2,0,3,1:T(8,128)}, u32[]{:S(2)}) copy-start(f32[8,2,512,64]{2,0,3,1:T(8,128)} %get-tuple-element.73) | copy-start | bytes 6291460
  280.8 6.1 %copy-start.11 = (f32[8,2,512,64]{2,0,3,1:T(8,128)S(1)}, f32[8,2,512,64]{2,0,3,1:T(8,128)}, u32[]{:S(2)}) copy-start(f32[8,2,512,64]{2,0,3,1:T(8,128)} %get-tuple-element.75) | copy-start | bytes 6291460
  280.8 6.1 %collective-permute-start.31 = (f32[8,2,514,1]{2,0,3,1:T(8,128)S(1)}, f32[8,2,514,1]{2,0,3,1:T(8,128)S(1)}, u32[]{:S(2)}, u32[]{:S(2)}) collective-permute-start(f32[8,2,514,1]{2,0,3,1:T(8,128)S(1)} %get-tuple-element.16), channel_id=1, source_target_pairs={{0,1},{1,2},{2,3},{3,4},{4,5},{5,6},{6,7},{7,8},{8,9},{9,10},{10,1... | collective-permute-start | bytes 98696 | tf_op jit(solution)/shard_map/ppermute | solution.py:32
  292.8 1.3 copy-start.4
  296.1 16.8 %copy-start.5 = (f32[8,2,512,64]{2,0,3,1:T(8,128)S(1)}, f32[8,2,512,64]{2,0,3,1:T(8,128)}, u32[]{:S(2)}) copy-start(f32[8,2,512,64]{2,0,3,1:T(8,128)} %copy-done.4) | copy-start | bytes 6291460
  297.9 89.2 %all-gather.2.cloned.1.call-start = ((), (), s32[]{:S(2)}) async-start(), calls=%async_computation.4 | async-start | bytes 8912896 | tf_op jit(solution)/shard_map/all_gather | solution.py:87
  312.6 138.6 %reduce-scatter.6.cloned.1.call-start = ((), (), s32[]{:S(2)}) async-start(), calls=%async_computation.3 | async-start | bytes 2228224 | tf_op jit(solution)/shard_map/reduce_scatter | solution.py:80
  312.9 47.4 %collective-permute-start.32 = (f32[8,2,512,64]{2,0,3,1:T(8,128)S(1)}, f32[8,2,512,64]{2,0,3,1:T(8,128)}, u32[]{:S(2)}, u32[]{:S(2)}) collective-permute-start(f32[8,2,512,64]{2,0,3,1:T(8,128)S(1)} %copy-done.5), channel_id=1, source_target_pairs={{0,16},{16,0},{1,17},{17,1},{2,18},{18,2},{3,19},{19,3},{4,20},{20... | collective-permute-start | bytes 6291464 | tf_op jit(solution)/shard_map/ppermute | solution.py:18
  370.7 93.3 %reduce-scatter.8.cloned.1.call-start = ((), (), s32[]{:S(2)}) async-start(), calls=%async_computation.5 | async-start | bytes 393216 | tf_op jit(solution)/shard_map/reduce_scatter | solution.py:90
  394.0 58.9 %copy-start.6 = (bf16[1024,128]{1,0:T(8,128)(2,1)S(1)}, bf16[1024,128]{1,0:T(8,128)(2,1)}, u32[]{:S(2)}) copy-start(bf16[1024,128]{1,0:T(8,128)(2,1)} %param.11) | copy-start | bytes 786436
Sparse Core Ops, SparseCore 0:
  298.0 11.9 reduce-scatter.9
  312.8 74.2 all-gather.1
  390.8 60.3 reduce-scatter.5
  453.3 10.6 reduce-scatter.7
